TPU v7x, 512 devices: a whole 4x8x8 slice. The times are simulated.
512 devices in a mesh: batch: 16 (over y, core), seq: 32 (over x, z).
Axes of the slice: x: 4, y: 8, z: 8, core: 2. Of those that a mesh axis runs over, the one named last changes fastest.
Arguments:
- tokens: bfloat16 [16, 16384, 768], P('batch', 'seq'), may hold values from -6 to 6
- slide_lengths: int32 [16], P('batch'), may hold values from 2048 to 16384, as said below
- conv_weight: float32 [5, 768], replicated, may hold values from -2.5 to 2.5
- norm_gain: float32 [768], replicated, may hold values from 0.1 to 1.9
- w_query: bfloat16 [768, 768], P('batch'), may hold values from -8 to 8
- w_keyvalue: bfloat16 [768, 1536], P('batch'), may hold values from -0.21875 to 0.21875
- w_out: bfloat16 [768, 768], P('batch'), may hold values from -0.625 to 0.625
Outputs:
- result: bfloat16 [16, 16384, 768], P('batch', 'seq')
Inputs may be any that keep to these rules, and one draw needn't show every extreme that they name: `slide_lengths`: some slide uses all 16384 token slots.
All inputs are finite; a program needn't handle non-finite values.
Results may differ from a plain program's by a relative error of at most 0.0055.
The roundings to bfloat16 on the way count: a program that leaves them out, or rounds other values in their place, can miss the bound.
Values may be sent and summed in bfloat16 or wider, within the bound.
A program may use at most 64 MiB of HBM per device.

v0:
```python
import math

import jax
import jax.numpy as jnp
from jax import lax
from jax.sharding import PartitionSpec as P

HEADS = 12
GROUP = 4
CONV_TAP_COUNT = 5
CONV_DILATION = 3


def with_halo(cells, sides, width):
    for axis, dim in sides:
        count = lax.axis_size(axis)
        ends = count - 1
        head = lax.slice_in_dim(cells, 0, width, axis=dim)
        tail = lax.slice_in_dim(cells, cells.shape[dim] - width, cells.shape[dim], axis=dim)
        cells = jnp.concatenate(
            [
                lax.ppermute(tail, axis, [(i, (i + 1) % count) for i in range(ends)]),
                cells,
                lax.ppermute(head, axis, [((i + 1) % count, i) for i in range(ends)]),
            ],
            axis=dim,
        )
    return cells


def partner_2(block, axis, stride):
    count = lax.axis_size(axis)
    route = []
    for low in range(count):
        high = low | 1 << stride
        if high != low and high < count:
            route += [(low, high), (high, low)]
    return lax.ppermute(block, axis, route)


def start_state(batch_count, row_count, head_size):
    return (
        jnp.full((batch_count, row_count), -1e30, jnp.float32),
        jnp.zeros((batch_count, row_count), jnp.float32),
        jnp.zeros((batch_count, row_count, head_size), jnp.float32),
    )


def absorb(carry_state, query_vectors, key_vectors, value_vectors, usable, part_count):

    def split_parts(array):
        return array.reshape((part_count, array.shape[0] // part_count) + array.shape[1:])

    def update(item_tuple):
        (
            running_max,
            running_sum,
            weighted_values,
            query_segment_block,
            key_segment_block,
            value_block,
            usable_block,
        ) = item_tuple
        score_matrix = jnp.einsum(
            "ftl,fhl->fth",
            query_segment_block,
            key_segment_block,
            preferred_element_type=jnp.float32,
        )
        score_matrix = jnp.where(usable_block[:, None, :], score_matrix, -1000000000.0)
        new_max = jnp.maximum(running_max, jnp.max(score_matrix, axis=-1))
        exponent = jnp.exp(score_matrix - new_max[..., None])
        factor = jnp.exp(running_max - new_max)
        new_sum = running_sum * factor + jnp.sum(exponent, axis=-1)
        new_weighted = weighted_values * factor[..., None] + jnp.einsum(
            "hcp,hpu->hcu",
            exponent.astype(jnp.bfloat16),
            value_block,
            preferred_element_type=jnp.float32,
        )
        return (new_max, new_sum, new_weighted)

    pieces = tuple(
        (
            split_parts(array)
            for array in carry_state + (query_vectors, key_vectors, value_vectors, usable)
        )
    )
    updated = lax.map(update, pieces)
    return tuple((array.reshape((-1,) + array.shape[2:]) for array in updated))


def finish(carry_state):
    running_max, running_sum, weighted_values = carry_state
    return (weighted_values / running_sum[..., None], running_max + jnp.log(running_sum))


def pick_rows(array, rate, head_count):
    grouped = array.reshape(head_count, array.shape[1] // rate, rate, array.shape[2])
    return jnp.stack([grouped[head, :, head % rate, :] for head in range(head_count)])


def spread_rows(outputs, log_total, rate, head_count):
    chosen = jnp.arange(rate)[None, :] == (jnp.arange(head_count) % rate)[:, None]
    full_out = jnp.where(chosen[:, None, :, None], outputs[:, :, None, :], 0.0).reshape(
        head_count, -1, outputs.shape[2]
    )
    full_log = jnp.where(chosen[:, None, :], log_total[:, :, None], -jnp.inf).reshape(
        head_count, -1
    )
    return (full_out, full_log)


def on_device(tokens, slide_lengths, conv_weight, norm_gain, w_query, w_keyvalue, w_out):
    tok_rows = tokens.shape[1]
    model_width = tokens.shape[2]
    head_count = HEADS
    head_size = model_width // head_count
    seq_count = lax.axis_size("seq")
    seq_index = lax.axis_index("seq")
    first_row = seq_index * tok_rows
    length = slide_lengths[0]
    position = first_row + jnp.arange(tok_rows, dtype=jnp.int32)
    live_rows = position < length
    masked = jnp.where(live_rows[:, None], tokens[0], jnp.zeros_like(tokens[0]))
    border_padding = CONV_DILATION * (CONV_TAP_COUNT // 2)
    padded = with_halo(masked, (("seq", 0),), border_padding)
    mixed_rows = masked.astype(jnp.float32)
    for filter_tap_index in range(CONV_TAP_COUNT):
        tap_shift_amount = border_padding + (filter_tap_index - CONV_TAP_COUNT // 2) * CONV_DILATION
        mixed_rows = mixed_rows + conv_weight[filter_tap_index] * padded[
            tap_shift_amount : tap_shift_amount + tok_rows
        ].astype(jnp.float32)
    average = jnp.mean(mixed_rows, axis=-1, keepdims=True)
    centered = mixed_rows - average
    variance = jnp.mean(centered * centered, axis=-1, keepdims=True)
    normed = (centered * lax.rsqrt(variance + 1e-05) * norm_gain).astype(jnp.bfloat16)
    piece_rows = (
        lax.all_gather(w_query, "batch", axis=0, tiled=True),
        lax.all_gather(w_keyvalue, "batch", axis=0, tiled=True),
    )
    columns = normed
    query_sum = jnp.dot(columns, piece_rows[0], preferred_element_type=jnp.float32)
    pair_sum = jnp.dot(columns, piece_rows[1], preferred_element_type=jnp.float32)
    query_vectors = (query_sum * (1.0 / math.sqrt(head_size))).astype(jnp.bfloat16)
    key_value = pair_sum.astype(jnp.bfloat16)
    query_heads = query_vectors.reshape(tok_rows, head_count, head_size).transpose(1, 0, 2)
    key_heads = (
        key_value[:, :model_width].reshape(tok_rows, head_count, head_size).transpose(1, 0, 2)
    )
    value_heads = (
        key_value[:, model_width:].reshape(tok_rows, head_count, head_size).transpose(1, 0, 2)
    )
    head_index = jnp.arange(head_count, dtype=jnp.int32)
    dense_usable = jnp.broadcast_to(live_rows[None, :], (head_count, tok_rows))
    dense_state = absorb(
        start_state(head_count, tok_rows, head_size),
        query_heads,
        key_heads,
        value_heads,
        dense_usable,
        3,
    )
    dense_out, dense_log = finish(dense_state)
    group_rows = tok_rows // GROUP
    group_offsets = head_index % GROUP
    group_queries = pick_rows(query_heads, GROUP, head_count)
    group_block = jnp.stack(
        [pick_rows(key_heads, GROUP, head_count), pick_rows(value_heads, GROUP, head_count)]
    )
    for bit_number in range(GROUP.bit_length() - 1):
        partner = partner_2(group_block, "seq", bit_number)
        upper_half = seq_index >> bit_number & 1 == 1
        group_block = jnp.where(
            upper_half,
            jnp.concatenate([partner, group_block], axis=2),
            jnp.concatenate([group_block, partner], axis=2),
        )
    group_first = seq_index // GROUP * GROUP * tok_rows
    block_steps = GROUP * jnp.arange(GROUP * group_rows, dtype=jnp.int32)
    block_usable = group_first + block_steps[None, :] + group_offsets[:, None] < length
    group_state = absorb(
        start_state(head_count, group_rows, head_size),
        group_queries,
        group_block[0],
        group_block[1],
        block_usable,
        3,
    )
    group_out, group_log = finish(group_state)
    group_out, group_log = spread_rows(group_out, group_log, GROUP, head_count)
    slide_rows = tok_rows // seq_count
    slide_offsets = head_index % seq_count
    slide_queries_own = pick_rows(query_heads, seq_count, head_count)
    slide_keys_own = pick_rows(key_heads, seq_count, head_count)
    slide_values_own = pick_rows(value_heads, seq_count, head_count)
    slide_pairs = jnp.stack([slide_keys_own, slide_values_own])
    piece_rows = lax.all_gather(slide_pairs, "seq", axis=2, tiled=True)
    count = piece_rows.shape[2]
    key_positions = seq_count * jnp.arange(count, dtype=jnp.int32)[None, :] + slide_offsets[:, None]
    slide_state = absorb(
        start_state(head_count, slide_rows, head_size),
        slide_queries_own,
        piece_rows[0],
        piece_rows[1],
        key_positions < length,
        1,
    )
    slide_out, slide_log = finish(slide_state)
    slide_out, slide_log = spread_rows(slide_out, slide_log, seq_count, head_count)
    highest = jnp.maximum(jnp.maximum(dense_log, group_log), slide_log)
    dense_factor = jnp.exp(dense_log - highest)
    group_factor = jnp.exp(group_log - highest)
    slide_factor = jnp.exp(slide_log - highest)
    numer = (
        dense_factor[..., None] * dense_out
        + group_factor[..., None] * group_out
        + slide_factor[..., None] * slide_out
    )
    denom = dense_factor + group_factor + slide_factor
    combined = jnp.where(live_rows[None, :, None], numer / denom[..., None], 0.0)
    attention = combined.transpose(1, 0, 2).reshape(tok_rows, model_width).astype(jnp.bfloat16)
    columns = attention
    projected = jnp.dot(
        columns,
        lax.all_gather(w_out, "batch", axis=0, tiled=True),
        preferred_element_type=jnp.float32,
    )
    return projected.astype(jnp.bfloat16).reshape(1, tok_rows, model_width)


def solution(mesh):
    return jax.shard_map(
        on_device,
        mesh=mesh,
        in_specs=(
            P("batch", "seq", None),
            P("batch"),
            P(),
            P(),
            P("batch", None),
            P("batch", None),
            P("batch", None),
        ),
        out_specs=P("batch", "seq", None),
        check_vma=False,
    )
```

profile of v0, /device:TPU:1, one launch (start us, length us, event | category | flops | bytes accessed | tf_op | source)
XLA Modules:
  0.0 283.2 jit_solution(16786506327512890809)
XLA Ops:
  8.0 1.3 bitcast_select_fusion.1
  9.3 4.8 %collective-permute-start = (bf16[6,768]{1,0:T(8,128)(2,1)S(1)}, bf16[6,768]{1,0:T(8,128)(2,1)S(1)}, u32[]{:S(2)}, u32[]{:S(2)}) collective-permute-start(bf16[6,768]{1,0:T(8,128)(2,1)S(1)} %get-tuple-element.344), channel_id=1, source_target_pairs={{0,1},{1,2},{2,3},{3,4},{4,5},{5,6},{6,7},{7,8},{8,9},{9,10},{10,1... | collective-permute-start | bytes 27656 | tf_op jit(solution)/shard_map/ppermute | solution.py:22
  14.1 1.3 collective-permute-start.1
  15.6 3.6 %collective-permute-done.1 = bf16[6,768]{1,0:T(8,128)(2,1)S(1)} collective-permute-done((bf16[6,768]{1,0:T(8,128)(2,1)S(1)}, bf16[6,768]{1,0:T(8,128)(2,1)S(1)}, u32[]{:S(2)}, u32[]{:S(2)}) %collective-permute-start.1) | collective-permute-done | bytes 9248 | tf_op jit(solution)/shard_map/ppermute | solution.py:24
  20.7 37.1 %all-gather.7.cloned.1.call-done = bf16[768,1536]{1,0:T(8,128)(2,1)} async-done(((bf16[48,1536]{1,0:T(8,128)(2,1)}), bf16[768,1536]{1,0:T(8,128)(2,1)}) %all-gather.7.cloned.1.call-update) | async-done | bytes 2359312 | tf_op jit(solution)/shard_map/all_gather | solution.py:140
  57.8 3.1 %convolution_convert_fusion = bf16[512,1536]{1,0:T(8,128)(2,1)S(1)} fusion(bf16[768,1536]{1,0:T(8,128)(2,1)} %all-gather.7.cloned.1.call-done, f32[512,768]{1,0:T(8,128)S(1)} %get-tuple-element.253, f32[768]{0:T(1024)S(1)} %copy-done.15, f32[512]{0:T(512)S(1)} %add_rsqrt_fusion, f32[512]{0:T(512)S(1)} %broadcast_multiply_fusion), kind=kOutput, calls=%fused_computation.64 | convolution fusion | flops 1210318848 | bytes 5512192 | tf_op jit(solution)/shard_map/dot_general | solution.py:144
  62.2 1.5 copy.1435
  64.8 1.4 copy.1421
  66.2 1.6 copy.1448
  72.3 27.5 %all-gather.5.cloned.1.call-done = bf16[768,768]{1,0:T(8,128)(2,1)} async-done(((bf16[48,768]{1,0:T(8,128)(2,1)}), bf16[768,768]{1,0:T(8,128)(2,1)}) %all-gather.5.cloned.1.call-update) | async-done | bytes 1179664 | tf_op jit(solution)/shard_map/all_gather | solution.py:139
  99.9 3.0 %multiply_convert_fusion = bf16[512,768]{1,0:T(8,128)(2,1)} fusion(bf16[768,768]{1,0:T(8,128)(2,1)} %all-gather.5.cloned.1.call-done, f32[512,768]{1,0:T(8,128)S(1)} %get-tuple-element.253, f32[768]{0:T(1024)S(1)} %copy-done.15, f32[512]{0:T(512)S(1)} %add_rsqrt_fusion, f32[512]{0:T(512)S(1)} %broadcast_multiply_fusion), kind=kOutput, calls=%fused_computation.72 | convolution fusion | flops 606339072 | bytes 3546112 | tf_op jit(solution)/shard_map/dot_general | solution.py:143
  102.8 1.4 copy.1419
  104.2 1.6 copy.1422
  105.9 1.7 fusion.77
  107.5 2.4 fusion.82
  117.5 2.4 fusion.79
  127.7 3.0 %fusion.81 = (bf16[1,128,1,64]{3,2,1,0:T(2,128)(2,1)S(1)}, bf16[1,128,1,64]{3,2,1,0:T(2,128)(2,1)S(1)}, bf16[1,128,1,64]{3,2,1,0:T(2,128)(2,1)S(1)}, bf16[1,128,...) fusion(bf16[12,128,4,64]{3,2,1,0:T(4,128)(2,1)} %bitcast.349), kind=kLoop, calls=%fused_computation.224 | loop fusion | bytes 393216 | tf_op jit(solution)/shard_map/slice | solution.py:100
  132.1 1.5 copy.1512
  133.6 1.5 copy.1513
  148.3 3.4 %collective-permute-start.2 = (bf16[2,12,128,64]{2,3,1,0:T(8,128)(2,1)S(1)}, bf16[2,12,128,64]{2,3,1,0:T(8,128)(2,1)S(1)}, u32[]{:S(2)}, u32[]{:S(2)}) collective-permute-start(bf16[2,12,128,64]{2,3,1,0:T(8,128)(2,1)S(1)} %pad_maximum_fusion.2), channel_id=1, source_target_pairs={{0,1},{1,0},{2,3},{3,2},{4,5},{5,4},{6,7},{7,6},{8,9},{9,8},{10,11... | collective-permute-start | bytes 1179656 | tf_op jit(solution)/shard_map/ppermute | solution.py:38
  152.3 9.9 %collective-permute-done.2 = bf16[2,12,128,64]{2,3,1,0:T(8,128)(2,1)S(1)} collective-permute-done((bf16[2,12,128,64]{2,3,1,0:T(8,128)(2,1)S(1)}, bf16[2,12,128,64]{2,3,1,0:T(8,128)(2,1)S(1)}, u32[]{:S(2)}, u32[]{:S(2)}) %collective-permute-start.2) | collective-permute-done | bytes 393248 | tf_op jit(solution)/shard_map/ppermute | solution.py:38
  163.4 4.9 %collective-permute-start.3 = (bf16[2,12,256,64]{2,3,1,0:T(8,128)(2,1)}, bf16[2,12,256,64]{2,3,1,0:T(8,128)(2,1)}, u32[]{:S(2)}, u32[]{:S(2)}) collective-permute-start(bf16[2,12,256,64]{2,3,1,0:T(8,128)(2,1)} %maximum_select_fusion.1), channel_id=1, source_target_pairs={{0,2},{2,0},{1,3},{3,1},{4,6},{6,4},{5,7},{7,5},{8,10},{10,8},{9,1... | collective-permute-start | bytes 2359304 | tf_op jit(solution)/shard_map/ppermute | solution.py:38
  168.4 13.2 %while.10 = (s32[]{:T(128)}, f32[3,4,512]{2,1,0:T(4,128)S(1)}, f32[3,4,512]{2,1,0:T(4,128)S(1)}, f32[3,4,512,64]{2,3,1,0:T(8,128)}, pred[3,4,512]{2,1,0:T(4,128)...) while((s32[]{:T(128)}, f32[3,4,512]{2,1,0:T(4,128)S(1)}, ...), condition=%wide.region_5.6_spmd, body=%wide.region_2.5_spmd.sunk | while | flops 276965376 | bytes 14004325 | solution.py:89
  168.5 1.5 select_reduce_fusion.2
  170.0 1.9 fusion.105
  172.9 1.5 select_reduce_fusion.2
  174.4 1.9 fusion.105
  177.2 1.5 select_reduce_fusion.2
  178.8 1.9 fusion.105
  182.9 2.1 copy.1481
  185.0 27.4 %collective-permute-done.3 = bf16[2,12,256,64]{2,3,1,0:T(8,128)(2,1)} collective-permute-done((bf16[2,12,256,64]{2,3,1,0:T(8,128)(2,1)}, bf16[2,12,256,64]{2,3,1,0:T(8,128)(2,1)}, u32[]{:S(2)}, u32[]{:S(2)}) %collective-permute-start.3) | collective-permute-done | bytes 786464 | tf_op jit(solution)/shard_map/ppermute | solution.py:38
  212.3 2.6 maximum_select_fusion
  216.2 11.3 %while.11 = (s32[]{:T(128)}, f32[3,4,128]{2,1,0:T(4,128)S(1)}, f32[3,4,128]{2,1,0:T(4,128)S(1)}, f32[3,4,128,64]{2,3,1,0:T(8,128)}, pred[3,4,512]{2,1,0:T(4,128)...) while((s32[]{:T(128)}, f32[3,4,128]{2,1,0:T(4,128)S(1)}, ...), condition=%wide.region_9.10_spmd, body=%wide.region_6.9_spmd.sunk | while | flops 68717056 | bytes 3899493 | solution.py:89
  216.2 1.4 fusion.108
  217.6 2.0 fusion.111
  220.0 1.4 fusion.108
  221.4 2.0 fusion.111
  223.7 1.4 fusion.108
  225.1 2.0 fusion.111
  230.6 9.3 %fusion.74 = (bf16[1,12,512,64]{3,0,1,2:T(2,128)(2,1)}, bf16[1,12,512,64]{3,0,1,2:T(2,128)(2,1)}) fusion(bf16[2,12,512,64]{3,0,1,2:T(2,128)(2,1)} %all-gather.9.cloned.1.call-done), kind=kLoop, calls=%fused_computation.217 | loop fusion | bytes 3145728 | tf_op jit(solution)/shard_map/slice | solution.py:205
  239.9 7.9 %copy.1535 = bf16[1,12,512,64]{2,3,1,0:T(8,128)(2,1)} copy(bf16[1,12,512,64]{3,0,1,2:T(2,128)(2,1)} %get-tuple-element.267) | data formatting | bytes 1572864
  247.8 7.9 %copy.1536 = bf16[1,12,512,64]{2,3,1,0:T(8,128)(2,1)} copy(bf16[1,12,512,64]{3,0,1,2:T(2,128)(2,1)} %get-tuple-element.266) | data formatting | bytes 1572864
  255.7 1.4 fusion.84
  258.8 1.6 broadcast_in_dim.237
  261.3 1.5 fusion.58
  263.6 8.3 %fusion.52 = bf16[12,512,64]{2,1,0:T(8,128)(2,1)} fusion(f32[12,512,64]{2,1,0:T(8,128)S(1)} %bitcast.338, f32[3,4,512,64]{3,2,1,0:T(8,128)S(1)} %copy.1481, f32[12,512]{1,0:T(8,128)S(1)} %get-tuple-element.248, f32[12,16,64]{2,1,0:T(8,128)S(1)} %fusion.58, f32[12,512]{1,0:T(8,128)S(1)} %get-tuple-element.251, f32[12,512]{1,0:T(8,128)S(1)} %get-tuple-element.249, ...), kind=kLoop, calls=%fused_computation.63 | loop fusion | flops 4325376 | bytes 4116992 | tf_op jit(solution)/shard_map/convert_element_type | solution.py:222
  272.0 1.7 copy.1485
  273.7 3.0 %fusion.57 = bf16[1,512,768]{2,1,0:T(8,128)(2,1)} fusion(bf16[512,768]{0,1:T(8,128)(2,1)S(1)} %bitcast.359, bf16[768,768]{1,0:T(8,128)(2,1)} %all-gather.11.cloned.1.call-done), kind=kOutput, calls=%fused_computation.76 | convolution fusion | flops 604372992 | bytes 2752512 | tf_op jit(solution)/shard_map/dot_general | solution.py:224
  (225 shorter events, 53.4 us)
Async XLA Ops:
  6.5 9.0 %copy-start.9 = (f32[5,768]{1,0:T(8,128)S(1)}, f32[5,768]{1,0:T(8,128)}, u32[]{:S(2)}) copy-start(f32[5,768]{1,0:T(8,128)} %param.13) | copy-start | bytes 46084
  6.5 51.2 %all-gather.7.cloned.1.call-start = ((), (), s32[]{:S(2)}) async-start(), calls=%async_computation.1 | async-start | bytes 2506752 | tf_op jit(solution)/shard_map/all_gather | solution.py:140
  7.3 92.6 %all-gather.5.cloned.1.call-start = ((), (), s32[]{:S(2)}) async-start(), calls=%async_computation | async-start | bytes 1253376 | tf_op jit(solution)/shard_map/all_gather | solution.py:139
  8.0 7.5 %copy-start.12 = (pred[512]{0:T(512)(128)(4,1)}, pred[512]{0:T(512)(128)(4,1)S(1)}, u32[]{:S(2)}) copy-start(pred[512]{0:T(512)(128)(4,1)S(1)} %add_compare_fusion.2) | copy-start | bytes 1540
  9.3 6.3 %collective-permute-start = (bf16[6,768]{1,0:T(8,128)(2,1)S(1)}, bf16[6,768]{1,0:T(8,128)(2,1)S(1)}, u32[]{:S(2)}, u32[]{:S(2)}) collective-permute-start(bf16[6,768]{1,0:T(8,128)(2,1)S(1)} %get-tuple-element.344), channel_id=1, source_target_pairs={{0,1},{1,2},{2,3},{3,4},{4,5},{5,6},{6,7},{7,8},{8,9},{9,10},{10,1... | collective-permute-start | bytes 27656 | tf_op jit(solution)/shard_map/ppermute | solution.py:22
  14.1 5.1 %collective-permute-start.1 = (bf16[6,768]{1,0:T(8,128)(2,1)S(1)}, bf16[6,768]{1,0:T(8,128)(2,1)S(1)}, u32[]{:S(2)}, u32[]{:S(2)}) collective-permute-start(bf16[6,768]{1,0:T(8,128)(2,1)S(1)} %get-tuple-element.345), channel_id=1, source_target_pairs={{1,0},{2,1},{3,2},{4,3},{5,4},{6,5},{7,6},{8,7},{9,8},{10,9},{11,1... | collective-permute-start | bytes 27656 | tf_op jit(solution)/shard_map/ppermute | solution.py:24
  15.4 215.2 %all-gather.9.cloned.1.call-start = ((), (), s32[]{:S(2)}) async-start(), calls=%async_computation.2 | async-start | bytes 3244032 | tf_op jit(solution)/shard_map/all_gather | solution.py:198
  19.2 38.6 %copy-start.15 = (f32[768]{0:T(1024)S(1)}, f32[768]{0:T(1024)}, u32[]{:S(2)}) copy-start(f32[768]{0:T(1024)} %param.14) | copy-start | bytes 9220
  69.9 203.8 %all-gather.11.cloned.1.call-start = ((), (), s32[]{:S(2)}) async-start(), calls=%async_computation.3 | async-start | bytes 1253376 | tf_op jit(solution)/shard_map/all_gather | solution.py:226
  117.4 2.5 copy-start.4
  135.9 16.4 %copy-start.3 = (bf16[1,128,1,64]{1,3,2,0:T(8,128)(2,1)S(1)}, bf16[1,128,1,64]{1,3,2,0:T(8,128)(2,1)}, u32[]{:S(2)}) copy-start(bf16[1,128,1,64]{1,3,2,0:T(8,128)(2,1)} %copy.1434) | copy-start | bytes 49156
  136.6 15.1 %copy-start.6 = (bf16[1,16,1,64]{3,2,1,0:T(2,128)(2,1)S(1)}, bf16[1,16,1,64]{3,2,1,0:T(2,128)(2,1)}, u32[]{:S(2)}) copy-start(bf16[1,16,1,64]{3,2,1,0:T(2,128)(2,1)} %get-tuple-element.292) | copy-start | bytes 6148
  137.3 31.1 %copy-start.13 = (pred[512]{0:T(512)(128)(4,1)S(1)}, pred[512]{0:T(512)(128)(4,1)}, u32[]{:S(2)}) copy-start(pred[512]{0:T(512)(128)(4,1)} %copy-done.12) | copy-start | bytes 1540
  137.3 31.1 %copy-start.7 = (f32[3,4,512]{2,1,0:T(4,128)S(1)}, f32[3,4,512]{2,1,0:T(4,128)}, u32[]{:S(2)}) copy-start(f32[3,4,512]{2,1,0:T(4,128)} %custom-call.6) | copy-start | bytes 73732
  137.3 31.1 %copy-start.8 = (f32[3,4,512]{2,1,0:T(4,128)S(1)}, f32[3,4,512]{2,1,0:T(4,128)}, u32[]{:S(2)}) copy-start(f32[3,4,512]{2,1,0:T(4,128)} %custom-call.7) | copy-start | bytes 73732
  148.3 13.9 %collective-permute-start.2 = (bf16[2,12,128,64]{2,3,1,0:T(8,128)(2,1)S(1)}, bf16[2,12,128,64]{2,3,1,0:T(8,128)(2,1)S(1)}, u32[]{:S(2)}, u32[]{:S(2)}) collective-permute-start(bf16[2,12,128,64]{2,3,1,0:T(8,128)(2,1)S(1)} %pad_maximum_fusion.2), channel_id=1, source_target_pairs={{0,1},{1,0},{2,3},{3,2},{4,5},{5,4},{6,7},{7,6},{8,9},{9,8},{10,11... | collective-permute-start | bytes 1179656 | tf_op jit(solution)/shard_map/ppermute | solution.py:38
  163.4 48.9 %collective-permute-start.3 = (bf16[2,12,256,64]{2,3,1,0:T(8,128)(2,1)}, bf16[2,12,256,64]{2,3,1,0:T(8,128)(2,1)}, u32[]{:S(2)}, u32[]{:S(2)}) collective-permute-start(bf16[2,12,256,64]{2,3,1,0:T(8,128)(2,1)} %maximum_select_fusion.1), channel_id=1, source_target_pairs={{0,2},{2,0},{1,3},{3,1},{4,6},{6,4},{5,7},{7,5},{8,10},{10,8},{9,1... | collective-permute-start | bytes 2359304 | tf_op jit(solution)/shard_map/ppermute | solution.py:38
  214.9 1.3 copy-start.10
  214.9 1.3 copy-start.11
  247.8 7.9 %copy-start.5 = (pred[12,512]{1,0:T(8,128)(4,1)S(1)}, pred[12,512]{1,0:T(8,128)(4,1)}, u32[]{:S(2)}) copy-start(pred[12,512]{1,0:T(8,128)(4,1)} %add_compare_fusion) | copy-start | bytes 18436
  260.4 2.5 copy-start
  262.9 0.8 copy-start.1
  262.9 0.8 copy-start.2
  262.9 0.7 copy-start.14
Sparse Core Ops, SparseCore 0:
  9.5 48.2 all-gather.6
  59.9 39.9 all-gather.4
  103.0 101.3 all-gather.8
  206.4 41.1 all-gather.10
where the time goes:
time: 286 us; the launch traced here: 283 us
  waiting for transfers between devices  107 us (37%)
  local copies, waits for them, and re-layouts  92.1 us (32%)
  matrix products  32.4 us (11%)
  other arithmetic  22.6 us (8%)
  between operations  14.6 us (5%)
  starting transfers between devices  14.5 us (5%)
    unnamed x112, local copies, waits for them, and re-layouts  38.8 us
    ppermute x2, waiting for transfers between devices, partner_2(): return lax.ppermute(block, axis, route)  37.3 us
    all_gather x1, waiting for transfers between devices, on_device(): lax.all_gather(w_keyvalue, 'batch', axis=0, tiled=True)  37.1 us
    all_gather x1, waiting for transfers between devices, on_device(): lax.all_gather(w_query, 'batch', axis=0, tiled=True)  27.5 us
    slice x30, local copies, waits for them, and re-layouts, pick_rows(): grouped[head, :, head % rate, :]  21 us
    dot_general x7, matrix products, update(): jnp.einsum('hcp,hpu->hcu', exponent.astype(jnp.bfloat16), value_block, pr...  13.2 us
    dot_general x7, matrix products, update(): jnp.einsum('ftl,fhl->fth', query_segment_block, key_segment_block, prefer...  10.1 us
    slice x1, local copies, waits for them, and re-layouts, on_device(): piece_rows[1]  9.28 us
  transfers between devices with their start and end apart: 8, of which 5 were waited for; matrix products, arithmetic and copies ran while one was open for 51% of the time, Pallas kernels for 0%

commit v1 on v0

v1 whole, which is shorter than its diff:
```python
import jax
import jax.numpy as jnp
from jax import lax
from jax.experimental import pallas as pl
from jax.experimental.pallas import tpu as pltpu
from jax.sharding import PartitionSpec as P

HEADS = 12
HEAD = 64
D = 768
ROWS = 512
TAPS = 5
DIL = 3
NY = 8
NX = 4
NZ = 8
SH = 48
CW = 640
PAD = 16
NEG = -1e9
F32 = jnp.float32
BF = jnp.bfloat16
MESH = pl.DeviceIdType.MESH


def lanes(shape):
    return lax.broadcasted_iota(jnp.int32, shape, len(shape) - 1)


def dot_nt(a, b):
    return lax.dot_general(a, b, (((1,), (1,)), ((), ())), preferred_element_type=F32)


def softmax_block(q, kv, bias):
    s = dot_nt(q, kv) + bias
    m = jnp.max(s, axis=1, keepdims=True)
    e = jnp.exp(s - m)
    total = jnp.sum(e, axis=1, keepdims=True)
    o = jnp.dot(e.astype(BF), kv, preferred_element_type=F32)
    return o / total, m + jnp.log(total)


def attend3(qa, qb, kv, bias):
    low = lanes(qa.shape) < HEAD
    zero = jnp.zeros_like(qa)
    o0, l0 = softmax_block(jnp.where(low, qa, zero), kv(0), bias)
    o1, l1 = softmax_block(jnp.where(low, zero, qa), kv(1), bias)
    o2, l2 = softmax_block(qb, kv(2), bias)
    flow = lanes(o0.shape) < HEAD
    return (
        jnp.where(flow, o1, o0),
        jnp.where(flow, 0.0, o2),
        jnp.where(flow, l1, l0),
        jnp.broadcast_to(l2, o2.shape),
    )


def split_log(value, lane):
    hi = value.astype(BF).astype(F32)
    rest = value - hi
    mid = rest.astype(BF).astype(F32)
    lo = rest - mid
    place = lane % 16
    return jnp.where(
        place == 0, hi, jnp.where(place == 1, mid, jnp.where(place == 2, lo, 0.0))
    )


def kernel(
    tok_ref,
    len_ref,
    cw_ref,
    gain_ref,
    wq_ref,
    wkv_ref,
    wo_ref,
    out_ref,
    wfull,
    woutf,
    woutp,
    xp,
    hl,
    hr,
    xn,
    kvq,
    mid,
    slp,
    sl,
    oret,
    ret,
    sret,
    srt,
    attn,
    dout,
    dlog,
    outf,
    ring_s,
    ring_r,
    sib_s,
    sib_r,
    halo_s,
    halo_r,
    a2a_s,
    a2a_r,
    slz_s,
    slz_r,
    slo_s,
    slo_r,
    slx_s,
    slx_r,
    ret_s,
    ret_r,
    srt_s,
    srt_r,
):
    b = lax.axis_index("batch")
    q = lax.axis_index("seq")
    y = b // 2
    c = b % 2
    x = q // NZ
    z = q % NZ
    zr = z % 4
    zg = z // 4
    length = len_ref[0]
    first = q * ROWS

    barrier = pltpu.get_barrier_semaphore()
    friends = [
        (2 * ((y + 1) % NY) + c, q),
        (2 * ((y + NY - 1) % NY) + c, q),
        (2 * y + 1 - c, q),
        (b, (q + 1) % 32),
        (b, (q + 31) % 32),
    ]
    friends += [(b, x * NZ + (z + i) % NZ) for i in range(1, NZ)]
    friends += [(b, ((x + i) % NX) * NZ + z) for i in range(1, NX)]
    for friend in friends:
        pl.semaphore_signal(barrier, inc=1, device_id=friend, device_id_type=MESH)

    own_rows = pl.ds(pl.multiple_of(b * SH, 16), SH)
    wlane = lanes((SH, 128)) < HEAD

    def half(ref, col, upper):
        block = ref[:, (col // 128) * 128 : (col // 128) * 128 + 128].astype(F32)
        if (col % 128 == HEAD) != upper:
            block = pltpu.roll(block, HEAD, 1)
        return block

    def place(r, i, low, high):
        wfull[r, own_rows, 128 * i : 128 * i + 128] = jnp.where(wlane, low, high).astype(BF)

    for r in range(4):
        h0, h1, h2 = HEAD * r, HEAD * (r + 4), HEAD * (r + 8)
        place(r, 0, half(wkv_ref, h0, False), half(wkv_ref, D + h0, True))
        place(r, 1, half(wkv_ref, D + h1, False), half(wkv_ref, h1, True))
        place(r, 2, half(wkv_ref, h2, False), half(wkv_ref, D + h2, True))
        place(r, 3, half(wq_ref, h0, False), half(wq_ref, h1, True))
        place(r, 4, half(wq_ref, h2, False), jnp.zeros((SH, 128), F32))
    woutf[own_rows, :] = wo_ref[...]

    def cls(g):
        return (zr + g + 1) % 4

    way = 1 - 2 * c

    def shard(ch, yo, co):
        rows = pl.ds(pl.multiple_of((2 * yo + co) * SH, 16), SH)
        if ch < 4:
            return wfull.at[cls(ch), rows, :]
        return woutf.at[rows, :]

    def ring_copy(ch, long, k):
        d = way if long else -way
        part = shard(ch, (y + NY - k * d) % NY, c)
        i = k if long else 4 + k
        return pltpu.make_async_remote_copy(
            src_ref=part,
            dst_ref=part,
            send_sem=ring_s.at[ch, i],
            recv_sem=ring_r.at[ch, i],
            device_id=(2 * ((y + NY + d) % NY) + c, q),
            device_id_type=MESH,
        )

    def sib_copy(ch, i):
        step = -i * way if i <= 4 else (i - 4) * way
        part = shard(ch, (y + NY + step) % NY, c)
        return pltpu.make_async_remote_copy(
            src_ref=part,
            dst_ref=part,
            send_sem=sib_s.at[ch, i],
            recv_sem=sib_r.at[ch, i],
            device_id=(2 * y + 1 - c, q),
            device_id_type=MESH,
        )

    def event(ch, k):
        if ch > 4:
            return
        if k == 0:
            ring_copy(ch, True, 0).start()
            ring_copy(ch, False, 0).start()
            sib_copy(ch, 0).start()
            return
        ring_copy(ch, True, k - 1).wait_recv()
        if k <= 3:
            ring_copy(ch, True, k).start()
        sib_copy(ch, k).start()
        if k <= 3:
            ring_copy(ch, False, k - 1).wait_recv()
            if k <= 2:
                ring_copy(ch, False, k).start()
            sib_copy(ch, 4 + k).start()

    def complete(ch):
        for i in range(8):
            sib_copy(ch, i).wait_recv()

    def halo_copy(right):
        if right:
            src, dst, i, to = tok_ref.at[0, pl.ds(ROWS - PAD, PAD), :], hl, 0, (q + 1) % 32
        else:
            src, dst, i, to = tok_ref.at[0, pl.ds(0, PAD), :], hr, 1, (q + 31) % 32
        return pltpu.make_async_remote_copy(
            src_ref=src,
            dst_ref=dst,
            send_sem=halo_s.at[i],
            recv_sem=halo_r.at[i],
            device_id=(b, to),
            device_id_type=MESH,
        )

    pl.semaphore_wait(barrier, len(friends))
    event(0, 0)
    halo_copy(True).start()
    halo_copy(False).start()
    event(1, 0)

    for i in range(6):
        cols = slice(128 * i, 128 * i + 128)
        pos = first + lax.broadcasted_iota(jnp.int32, (ROWS, 128), 0)
        xp[i, PAD : PAD + ROWS, :] = jnp.where(
            pos < length, tok_ref[0, :, cols].astype(F32), 0.0
        )

    def conv(s):
        parts = []
        for i in range(6):
            cols = slice(128 * i, 128 * i + 128)
            acc = xp[i, pl.ds(PAD + s, 16, stride=32), :]
            for t in range(TAPS):
                tap = xp[i, pl.ds(PAD + s + (t - TAPS // 2) * DIL, 16, stride=32), :]
                acc = acc + cw_ref[t : t + 1, cols] * tap
            parts.append(acc)
        total = parts[0]
        for part in parts[1:]:
            total = total + part
        mean = jnp.sum(total, axis=1, keepdims=True) * (1.0 / D)
        parts = [part - mean for part in parts]
        square = parts[0] * parts[0]
        for part in parts[1:]:
            square = square + part * part
        scale = lax.rsqrt(jnp.sum(square, axis=1, keepdims=True) * (1.0 / D) + 1e-5)
        row = pl.multiple_of(((s % 4) * 8 + s // 4) * 16, 16)
        for i in range(6):
            cols = slice(128 * i, 128 * i + 128)
            xn[pl.ds(row, 16), cols] = (parts[i] * scale * gain_ref[:, cols]).astype(BF)

    def conv_range(lo, hi):
        def step(s, carry):
            conv(s)
            return carry

        lax.fori_loop(lo, hi, step, 0)

    conv_range(6, 16)
    event(0, 1)
    conv_range(16, 26)
    event(0, 2)
    event(1, 1)
    halo_copy(True).wait_recv()
    halo_copy(False).wait_recv()
    for i in range(6):
        cols = slice(128 * i, 128 * i + 128)
        off = lax.broadcasted_iota(jnp.int32, (PAD, 128), 0)
        left = first - PAD + off
        right = first + ROWS + off
        left_ok = jnp.where(left >= 0, left, length) < length
        xp[i, 0:PAD, :] = jnp.where(left_ok, hl[:, cols].astype(F32), 0.0)
        xp[i, PAD + ROWS : 2 * PAD + ROWS, :] = jnp.where(
            right < length, hr[:, cols].astype(F32), 0.0
        )
    conv_range(0, 6)
    event(0, 3)
    event(1, 2)
    event(2, 0)
    conv_range(26, 32)
    event(0, 4)
    complete(0)

    def project(g):
        cg = cls(g)

        def step(i, carry):
            rows = pl.ds(pl.multiple_of(i * 256, 256), 256)
            res = jnp.dot(xn[rows, :], wfull[cg], preferred_element_type=F32)
            res = jnp.where(lanes(res.shape) < 384, res, res * (1.0 / 8.0))
            kvq[g, rows, :] = res.astype(BF)
            return carry

        lax.fori_loop(0, 2, step, 0)

    def cls_rows(g):
        return pl.ds(pl.multiple_of(cls(g) * 128, 128), 128)

    def a2a_copy(g):
        return pltpu.make_async_remote_copy(
            src_ref=kvq.at[g, cls_rows(g), :],
            dst_ref=mid.at[zr],
            send_sem=a2a_s.at[g],
            recv_sem=a2a_r.at[g],
            device_id=(b, x * NZ + zg * 4 + cls(g)),
            device_id_type=MESH,
        )

    def slz_copy(g):
        return pltpu.make_async_remote_copy(
            src_ref=slp.at[g],
            dst_ref=sl.at[x, z],
            send_sem=slz_s.at[g],
            recv_sem=slz_r.at[g],
            device_id=(b, x * NZ + zg * 4 + cls(g)),
            device_id_type=MESH,
        )

    def slo_copy(g):
        return pltpu.make_async_remote_copy(
            src_ref=slp.at[g],
            dst_ref=sl.at[x, z],
            send_sem=slo_s.at[g],
            recv_sem=slo_r.at[g],
            device_id=(b, x * NZ + (1 - zg) * 4 + cls(g)),
            device_id_type=MESH,
        )

    def slx_copy(i):
        return pltpu.make_async_remote_copy(
            src_ref=sl.at[x],
            dst_ref=sl.at[x],
            send_sem=slx_s.at[i],
            recv_sem=slx_r.at[i],
            device_id=(b, ((x + i + 1) % NX) * NZ + z),
            device_id_type=MESH,
        )

    def back(g):
        return (b, x * NZ + zg * 4 + (zr + 3 - g) % 4)

    def ret_copy(g):
        return pltpu.make_async_remote_copy(
            src_ref=oret.at[g],
            dst_ref=ret.at[g],
            send_sem=ret_s.at[g],
            recv_sem=ret_r.at[g],
            device_id=back(g),
            device_id_type=MESH,
        )

    def srt_copy(g):
        return pltpu.make_async_remote_copy(
            src_ref=sret.at[g],
            dst_ref=srt.at[g],
            send_sem=srt_s.at[g],
            recv_sem=srt_r.at[g],
            device_id=back(g),
            device_id_type=MESH,
        )

    def send_class(g):
        cg = cls(g)
        for u in range(3):
            rows = pl.ds(pl.multiple_of(cg * 128 + 16 * u, 16), 16)
            tile = kvq[g, rows, 128 * u : 128 * u + 128]
            slp[g, u] = tile
            if g == 3:
                sl[x, z, u] = tile
        slo_copy(g).start()
        if g < 3:
            slz_copy(g).start()
            a2a_copy(g).start()
        else:
            mid[zr] = kvq[g, cls_rows(g), :]

    key = lax.broadcasted_iota(jnp.int32, (1, ROWS), 1)
    inner = 32 * (key % 16) + 4 * ((key // 16) % 8)
    dense_bias = jnp.where(first + inner + key // 128 < length, 0.0, NEG)

    def live(r, width):
        row = lax.broadcasted_iota(jnp.int32, (128, width), 0)
        return first + 32 * (row % 16) + 4 * (row // 16) + r < length

    def dense(g, lo, hi):
        cg = cls(g)

        def step(i, carry):
            r = (cg + i) % 4
            rows = pl.ds(pl.multiple_of(r * 128, 128), 128)
            o0, o1, l0, l1 = attend3(
                kvq[g, rows, 384:512],
                kvq[g, rows, 512:640],
                lambda u: kvq[g, :, 128 * u : 128 * u + 128],
                dense_bias,
            )
            ok = live(r, 128)
            attn[cg, rows, 0:128] = jnp.where(ok, o0, 0.0).astype(BF)
            attn[cg, rows, 128:256] = jnp.where(ok, o1, 0.0).astype(BF)

            @pl.when(i == 0)
            def _():
                dout[g, :, 0:128] = o0
                dout[g, :, 128:256] = o1
                dlog[g, :, 0:128] = l0
                dlog[g, :, 128:256] = l1

            return carry

        lax.fori_loop(lo, hi, step, 0)

    for g in range(4):
        project(g)
        send_class(g)
        event(g + 1, 3)
        event(g + 2, 1)
        dense(g, 0, 2)
        event(g + 1, 4)
        event(g + 2, 2)
        event(g + 3, 0)
        dense(g, 2, 4)
        if g < 3:
            complete(g + 1)

    for g in range(3):
        slz_copy(g).wait_recv()
    for g in range(4):
        slo_copy(g).wait_recv()
    for i in range(3):
        slx_copy(i).start()

    for g in range(3):
        a2a_copy(g).wait_recv()
    group_first = (q // 4) * 4 * ROWS
    mid_bias = jnp.where(group_first + 512 * (key // 128) + inner + zr < length, 0.0, NEG)

    def mid_step(g, carry):
        m = (zr + 3 - g) % 4
        o0, o1, l0, l1 = attend3(
            mid[m, :, 384:512],
            mid[m, :, 512:640],
            lambda u: mid[:, :, 128 * u : 128 * u + 128].reshape(ROWS, 128),
            mid_bias,
        )
        lane = lanes(o0.shape)
        logs = jnp.where(
            lane < 16, pltpu.roll(l0, HEAD, 1), jnp.where(lane < 32, l0, l1)
        )
        logs = jnp.where(lane < 48, split_log(logs, lane), 0.0)
        oret[g, :, 0:128] = o0.astype(BF)
        oret[g, :, 128:256] = jnp.where(lane < HEAD, logs, o1).astype(BF)

        @pl.when(g < 3)
        def _():
            ret_copy(g).start()

        return carry

    lax.fori_loop(0, 4, mid_step, 0)

    for i in range(3):
        slx_copy(i).wait_recv()
    lane64 = lanes((64, 128))
    for u in range(3):
        low = 0 if u != 1 else HEAD
        blk = slice(384, 512) if u < 2 else slice(512, 640)
        qs = mid[:, 16 * u : 16 * u + 16, blk].reshape(64, 128)
        mine = jnp.where(low == 0, lane64, lane64 - HEAD + 128) % 128 < HEAD
        qs = jnp.where(mine, qs, jnp.zeros_like(qs))
        kv = sl[:, :, u].reshape(ROWS, 128)
        bias = jnp.where(32 * key + 4 * u + zr < length, 0.0, NEG)
        o, lg = softmax_block(qs, kv, bias)
        logs = split_log(jnp.broadcast_to(lg, o.shape), lane64)
        packed = jnp.where(mine, logs, o).astype(BF)
        for m in range(4):
            sret[(zr + 3 - m) % 4, u] = packed[16 * m : 16 * m + 16, :]
    for g in range(3):
        srt_copy(g).start()

    complete(4)
    for r in range(4):
        woutp[r, 0:64, :] = woutf[HEAD * (r + 4) : HEAD * (r + 5), :]
        woutp[r, 64:128, :] = woutf[HEAD * r : HEAD * (r + 1), :]
        woutp[r, 128:192, :] = jnp.zeros((64, D), BF)
        woutp[r, 192:256, :] = woutf[HEAD * (r + 8) : HEAD * (r + 9), :]

    def join(logs, outs):
        top = jnp.maximum(jnp.maximum(logs[0], logs[1]), logs[2])
        cs = [jnp.exp(lg - top) for lg in logs]
        num = cs[0] * outs[0] + cs[1] * outs[1] + cs[2] * outs[2]
        return num / (cs[0] + cs[1] + cs[2])

    lane128 = lanes((128, 128))
    lane16 = lanes((16, 128))
    flow = lane128 < HEAD

    def finish(g, mret, sr):
        cg = cls(g)
        rows = cls_rows(g)
        m0 = mret[:, 0:128].astype(F32)
        m1 = mret[:, 128:256].astype(F32)

        def mlog(u):
            hit = jnp.where((lane128 >= 16 * u) & (lane128 < 16 * u + 16), m1, 0.0)
            return jnp.sum(hit, axis=1, keepdims=True)

        ml0 = jnp.where(flow, mlog(1), mlog(0))
        ml1 = jnp.broadcast_to(mlog(2), (128, 128))
        souts = []
        slogs = []
        for u in range(3):
            val = sr(u).astype(F32)
            mine = lane16 >= HEAD if u == 1 else lane16 < HEAD
            first16 = lane16 % HEAD < 16
            lg = jnp.sum(jnp.where(mine & first16, val, 0.0), axis=1, keepdims=True)
            souts.append(jnp.where(mine, 0.0, val))
            slogs.append(jnp.where(mine, -1e30, lg))
        rest = jnp.zeros((80, 128), F32)
        z16 = jnp.zeros((16, 128), F32)
        n16 = jnp.full((16, 128), -1e30, F32)
        nrest = jnp.full((80, 128), -1e30, F32)
        s0 = jnp.concatenate([souts[0], souts[1], z16, rest], axis=0)
        sl0 = jnp.concatenate([slogs[0], slogs[1], n16, nrest], axis=0)
        s1 = jnp.concatenate([z16, z16, souts[2], rest], axis=0)
        sl1 = jnp.concatenate([n16, n16, slogs[2], nrest], axis=0)
        ok = live(cg, 128)
        a0 = join((dlog[g, :, 0:128], ml0, sl0), (dout[g, :, 0:128], m0, s0))
        a1 = join((dlog[g, :, 128:256], ml1, sl1), (dout[g, :, 128:256], m1, s1))
        a1 = jnp.where(flow, 0.0, a1)
        attn[cg, rows, 0:128] = jnp.where(ok, a0, 0.0).astype(BF)
        attn[cg, rows, 128:256] = jnp.where(ok, a1, 0.0).astype(BF)
        res = jnp.dot(attn[0, rows, :], woutp[0], preferred_element_type=F32)
        for r in range(1, 4):
            res = res + jnp.dot(attn[r, rows, :], woutp[r], preferred_element_type=F32)
        for v in range(8):
            for i in range(6):
                outf[i, pl.ds(4 * v + cg, 16, stride=32), :] = res[
                    16 * v : 16 * v + 16, 128 * i : 128 * i + 128
                ]

    finish(3, oret[3], lambda u: sret[3, u])
    for g in range(3):
        ret_copy(g).wait_recv()
        srt_copy(g).wait_recv()
        finish(g, ret[g], lambda u, g=g: srt[g, u])
    for i in range(6):
        out_ref[0, :, 128 * i : 128 * i + 128] = outf[i].astype(BF)

    for ch in range(5):
        for k in range(4):
            ring_copy(ch, True, k).wait_send()
        for k in range(3):
            ring_copy(ch, False, k).wait_send()
        for i in range(8):
            sib_copy(ch, i).wait_send()
    halo_copy(True).wait_send()
    halo_copy(False).wait_send()
    for g in range(3):
        a2a_copy(g).wait_send()
        slz_copy(g).wait_send()
        slx_copy(g).wait_send()
        ret_copy(g).wait_send()
        srt_copy(g).wait_send()
    for g in range(4):
        slo_copy(g).wait_send()


def on_device(tokens, slide_lengths, conv_weight, norm_gain, w_query, w_keyvalue, w_out):
    vmem = pl.BlockSpec(memory_space=pltpu.VMEM)
    dma = pltpu.SemaphoreType.DMA
    return pl.pallas_call(
        kernel,
        out_shape=jax.ShapeDtypeStruct((1, ROWS, D), BF),
        in_specs=[vmem, pl.BlockSpec(memory_space=pltpu.SMEM)] + [vmem] * 5,
        out_specs=vmem,
        scratch_shapes=[
            pltpu.VMEM((4, D, CW), BF),
            pltpu.VMEM((D, D), BF),
            pltpu.VMEM((4, 256, D), BF),
            pltpu.VMEM((6, ROWS + 2 * PAD, 128), F32),
            pltpu.VMEM((PAD, D), BF),
            pltpu.VMEM((PAD, D), BF),
            pltpu.VMEM((ROWS, D), BF),
            pltpu.VMEM((4, ROWS, CW), BF),
            pltpu.VMEM((4, 128, CW), BF),
            pltpu.VMEM((4, 3, 16, 128), BF),
            pltpu.VMEM((NX, NZ, 3, 16, 128), BF),
            pltpu.VMEM((4, 128, 256), BF),
            pltpu.VMEM((3, 128, 256), BF),
            pltpu.VMEM((4, 3, 16, 128), BF),
            pltpu.VMEM((3, 3, 16, 128), BF),
            pltpu.VMEM((4, ROWS, 256), BF),
            pltpu.VMEM((4, 128, 256), F32),
            pltpu.VMEM((4, 128, 256), F32),
            pltpu.VMEM((6, ROWS, 128), F32),
            dma((5, 7)),
            dma((5, 7)),
            dma((5, 8)),
            dma((5, 8)),
            dma((2,)),
            dma((2,)),
            dma((3,)),
            dma((3,)),
            dma((3,)),
            dma((3,)),
            dma((4,)),
            dma((4,)),
            dma((3,)),
            dma((3,)),
            dma((3,)),
            dma((3,)),
            dma((3,)),
            dma((3,)),
        ],
        compiler_params=pltpu.CompilerParams(
            collective_id=0, has_side_effects=True, vmem_limit_bytes=60 * 1024 * 1024
        ),
        name="layer",
    )(
        tokens,
        slide_lengths,
        conv_weight,
        norm_gain.reshape(1, D),
        w_query,
        w_keyvalue,
        w_out,
    )


def solution(mesh):
    return jax.shard_map(
        on_device,
        mesh=mesh,
        in_specs=(
            P("batch", "seq", None),
            P("batch"),
            P(),
            P(),
            P("batch", None),
            P("batch", None),
            P("batch", None),
        ),
        out_specs=P("batch", "seq", None),
        check_vma=False,
    )
```

time: 286 us -> 79.8 us (0.28)
  the two profiles are of different devices: /device:TPU:1 before, /device:TPU:64 now
where the time goes in v1:
time: 79.8 us; the launch traced here: 79.5 us
  Pallas kernels  75.5 us (95%)
  local copies, waits for them, and re-layouts  3.33 us (4%)
    pallas_call x1, Pallas kernels, on_device(): pl.pallas_call(kernel, out_shape=jax.ShapeDtypeStruct((1, ROWS, D), BF),...  75.5 us
    unnamed x1, local copies, waits for them, and re-layouts  2.06 us

profile of v1, /device:TPU:64, one launch (start us, length us, event | category | flops | bytes accessed | tf_op | source)
XLA Modules:
  0.0 79.5 jit_solution(7358517867803882758)
XLA Ops:
  0.7 1.3 %reshape.3.gain_ref = f32[1,768]{1,0:T(1,128)} reshape(f32[768]{0:T(1024)} %param.10) | data formatting | bytes 6144 | tf_op jit(solution)/shard_map/reshape | solution.py:640
  1.9 75.5 %layer.1 = bf16[1,512,768]{2,1,0:T(8,128)(2,1)} custom-call(bf16[1,512,768]{2,1,0:T(8,128)(2,1)} %tok_ref.1, s32[1]{0:T(128)S(6)} %copy.9.len_ref, f32[5,768]{1,0:T(8,128)} %cw_ref.1, f32[1,768]{1,0:T(1,128)} %reshape.3.gain_ref, bf16[48,768]{1,0:T(8,128)(2,1)} %wq_ref.1, bf16[48,1536]{1,0:T(8,128)(2,1)} %wkv_ref.1, bf16[48,768]{1,0:T(8,128)(2,1)} %wo_ref.1), custom_call_target="tpu_custom_call" | custom-call | tf_op jit(solution)/shard_map/layer/pallas_call | solution.py:588
  77.5 2.1 %copy.10 = bf16[1,512,768]{2,1,0:T(8,128)(2,1)} copy(bf16[1,512,768]{2,1,0:T(8,128)(2,1)} %layer.1) | data formatting | bytes 1572864

commit v2 on v1

--- a/solution.py
+++ b/solution.py
@@ -67,14 +67,21 @@
 
 
 def kernel(
+    tok_hbm,
+    len_ref,
+    cw_hbm,
+    gain_hbm,
+    wq_hbm,
+    wkv_hbm,
+    wo_hbm,
+    out_ref,
     tok_ref,
-    len_ref,
     cw_ref,
     gain_ref,
     wq_ref,
     wkv_ref,
     wo_ref,
-    out_ref,
+    in_s,
     wfull,
     woutf,
     woutp,
@@ -137,6 +144,24 @@
     for friend in friends:
         pl.semaphore_signal(barrier, inc=1, device_id=friend, device_id_type=MESH)
 
+    loads = [
+        pltpu.make_async_copy(src, dst, in_s.at[i])
+        for i, (src, dst) in enumerate(
+            (
+                (wkv_hbm, wkv_ref),
+                (wq_hbm, wq_ref),
+                (wo_hbm, wo_ref),
+                (tok_hbm, tok_ref),
+                (cw_hbm, cw_ref),
+                (gain_hbm, gain_ref),
+            )
+        )
+    ]
+    for load in loads:
+        load.start()
+    for load in loads[:3]:
+        load.wait()
+
     own_rows = pl.ds(pl.multiple_of(b * SH, 16), SH)
     wlane = lanes((SH, 128)) < HEAD
 
@@ -160,6 +185,14 @@
 
     def cls(g):
         return (zr + g + 1) % 4
+
+    def mask_tokens():
+        for j in range(16):
+            pos = first + 32 * j + lax.broadcasted_iota(jnp.int32, (32, 128), 0)
+            ok = pos < length
+            for i in range(6):
+                tile = tok_ref[0, 32 * j : 32 * j + 32, 128 * i : 128 * i + 128]
+                xp[i, 33 * j + 33 : 33 * j + 65, :] = jnp.where(ok, tile.astype(F32), 0.0)
 
     way = 1 - 2 * c
 
@@ -230,26 +263,23 @@
             device_id_type=MESH,
         )
 
+    for load in loads[3:]:
+        load.wait()
+    mask_tokens()
     pl.semaphore_wait(barrier, len(friends))
     event(0, 0)
     halo_copy(True).start()
     halo_copy(False).start()
     event(1, 0)
 
-    for i in range(6):
-        cols = slice(128 * i, 128 * i + 128)
-        pos = first + lax.broadcasted_iota(jnp.int32, (ROWS, 128), 0)
-        xp[i, PAD : PAD + ROWS, :] = jnp.where(
-            pos < length, tok_ref[0, :, cols].astype(F32), 0.0
-        )
-
     def conv(s):
         parts = []
         for i in range(6):
             cols = slice(128 * i, 128 * i + 128)
-            acc = xp[i, pl.ds(PAD + s, 16, stride=32), :]
+            acc = xp[i, pl.ds(33 + s, 16, stride=33), :]
             for t in range(TAPS):
-                tap = xp[i, pl.ds(PAD + s + (t - TAPS // 2) * DIL, 16, stride=32), :]
+                at = 32 + s + (t - TAPS // 2) * DIL
+                tap = xp[i, pl.ds(33 * (at // 32) + at % 32, 16, stride=33), :]
                 acc = acc + cw_ref[t : t + 1, cols] * tap
             parts.append(acc)
         total = parts[0]
@@ -264,20 +294,22 @@
         row = pl.multiple_of(((s % 4) * 8 + s // 4) * 16, 16)
         for i in range(6):
             cols = slice(128 * i, 128 * i + 128)
-            xn[pl.ds(row, 16), cols] = (parts[i] * scale * gain_ref[:, cols]).astype(BF)
+            xn[pl.ds(row, 16), cols] = (parts[i] * scale * gain_ref[cols].reshape(1, 128)).astype(BF)
 
     def conv_range(lo, hi):
         def step(s, carry):
-            conv(s)
+            conv(lo + 2 * s)
+            conv(lo + 2 * s + 1)
             return carry
 
-        lax.fori_loop(lo, hi, step, 0)
+        lax.fori_loop(0, (hi - lo) // 2, step, 0)
 
     conv_range(6, 16)
     event(0, 1)
     conv_range(16, 26)
+    event(1, 1)
+    event(2, 0)
     event(0, 2)
-    event(1, 1)
     halo_copy(True).wait_recv()
     halo_copy(False).wait_recv()
     for i in range(6):
@@ -286,16 +318,21 @@
         left = first - PAD + off
         right = first + ROWS + off
         left_ok = jnp.where(left >= 0, left, length) < length
-        xp[i, 0:PAD, :] = jnp.where(left_ok, hl[:, cols].astype(F32), 0.0)
-        xp[i, PAD + ROWS : 2 * PAD + ROWS, :] = jnp.where(
+        xp[i, 16:32, :] = jnp.where(left_ok, hl[:, cols].astype(F32), 0.0)
+        xp[i, 561:577, :] = jnp.where(
             right < length, hr[:, cols].astype(F32), 0.0
         )
     conv_range(0, 6)
+    event(1, 2)
+    event(2, 1)
     event(0, 3)
-    event(1, 2)
-    event(2, 0)
+    event(3, 0)
     conv_range(26, 32)
+    event(1, 3)
+    event(2, 2)
     event(0, 4)
+    event(3, 1)
+    event(4, 0)
     complete(0)
 
     def project(g):
@@ -399,43 +436,37 @@
         row = lax.broadcasted_iota(jnp.int32, (128, width), 0)
         return first + 32 * (row % 16) + 4 * (row // 16) + r < length
 
-    def dense(g, lo, hi):
+    def dense(g, i):
         cg = cls(g)
-
-        def step(i, carry):
-            r = (cg + i) % 4
-            rows = pl.ds(pl.multiple_of(r * 128, 128), 128)
-            o0, o1, l0, l1 = attend3(
-                kvq[g, rows, 384:512],
-                kvq[g, rows, 512:640],
-                lambda u: kvq[g, :, 128 * u : 128 * u + 128],
-                dense_bias,
-            )
+        r = (cg + i) % 4
+        rows = pl.ds(pl.multiple_of(r * 128, 128), 128)
+        o0, o1, l0, l1 = attend3(
+            kvq[g, rows, 384:512],
+            kvq[g, rows, 512:640],
+            lambda u: kvq[g, :, 128 * u : 128 * u + 128],
+            dense_bias,
+        )
+        if i == 0:
+            dout[g, :, 0:128] = o0
+            dout[g, :, 128:256] = o1
+            dlog[g, :, 0:128] = l0
+            dlog[g, :, 128:256] = l1
+        else:
             ok = live(r, 128)
             attn[cg, rows, 0:128] = jnp.where(ok, o0, 0.0).astype(BF)
             attn[cg, rows, 128:256] = jnp.where(ok, o1, 0.0).astype(BF)
 
-            @pl.when(i == 0)
-            def _():
-                dout[g, :, 0:128] = o0
-                dout[g, :, 128:256] = o1
-                dlog[g, :, 0:128] = l0
-                dlog[g, :, 128:256] = l1
-
-            return carry
-
-        lax.fori_loop(lo, hi, step, 0)
-
     for g in range(4):
         project(g)
         send_class(g)
-        event(g + 1, 3)
-        event(g + 2, 1)
-        dense(g, 0, 2)
         event(g + 1, 4)
-        event(g + 2, 2)
-        event(g + 3, 0)
-        dense(g, 2, 4)
+        dense(g, 0)
+        event(g + 2, 3)
+        dense(g, 1)
+        event(g + 3, 2)
+        dense(g, 2)
+        event(g + 4, 1)
+        dense(g, 3)
         if g < 3:
             complete(g + 1)
 
@@ -551,17 +582,11 @@
             res = res + jnp.dot(attn[r, rows, :], woutp[r], preferred_element_type=F32)
         for v in range(8):
             for i in range(6):
-                outf[i, pl.ds(4 * v + cg, 16, stride=32), :] = res[
+                outf[i, pl.ds(4 * v + cg, 16, stride=33), :] = res[
                     16 * v : 16 * v + 16, 128 * i : 128 * i + 128
                 ]
 
     finish(3, oret[3], lambda u: sret[3, u])
-    for g in range(3):
-        ret_copy(g).wait_recv()
-        srt_copy(g).wait_recv()
-        finish(g, ret[g], lambda u, g=g: srt[g, u])
-    for i in range(6):
-        out_ref[0, :, 128 * i : 128 * i + 128] = outf[i].astype(BF)
 
     for ch in range(5):
         for k in range(4):
@@ -576,25 +601,44 @@
         a2a_copy(g).wait_send()
         slz_copy(g).wait_send()
         slx_copy(g).wait_send()
+    for g in range(4):
+        slo_copy(g).wait_send()
+
+    for g in range(3):
+        ret_copy(g).wait_recv()
+        srt_copy(g).wait_recv()
+        finish(g, ret[g], lambda u, g=g: srt[g, u])
+    for j in range(16):
+        for i in range(6):
+            out_ref[0, 32 * j : 32 * j + 32, 128 * i : 128 * i + 128] = outf[
+                i, 33 * j : 33 * j + 32, :
+            ].astype(BF)
+    for g in range(3):
         ret_copy(g).wait_send()
         srt_copy(g).wait_send()
-    for g in range(4):
-        slo_copy(g).wait_send()
 
 
 def on_device(tokens, slide_lengths, conv_weight, norm_gain, w_query, w_keyvalue, w_out):
     vmem = pl.BlockSpec(memory_space=pltpu.VMEM)
+    hbm = pl.BlockSpec(memory_space=pl.ANY)
     dma = pltpu.SemaphoreType.DMA
     return pl.pallas_call(
         kernel,
         out_shape=jax.ShapeDtypeStruct((1, ROWS, D), BF),
-        in_specs=[vmem, pl.BlockSpec(memory_space=pltpu.SMEM)] + [vmem] * 5,
+        in_specs=[hbm, pl.BlockSpec(memory_space=pltpu.SMEM)] + [hbm] * 5,
         out_specs=vmem,
         scratch_shapes=[
+            pltpu.VMEM((1, ROWS, D), BF),
+            pltpu.VMEM((TAPS, D), F32),
+            pltpu.VMEM((D,), F32),
+            pltpu.VMEM((SH, D), BF),
+            pltpu.VMEM((SH, 2 * D), BF),
+            pltpu.VMEM((SH, D), BF),
+            dma((6,)),
             pltpu.VMEM((4, D, CW), BF),
             pltpu.VMEM((D, D), BF),
             pltpu.VMEM((4, 256, D), BF),
-            pltpu.VMEM((6, ROWS + 2 * PAD, 128), F32),
+            pltpu.VMEM((6, 33 * 18, 128), F32),
             pltpu.VMEM((PAD, D), BF),
             pltpu.VMEM((PAD, D), BF),
             pltpu.VMEM((ROWS, D), BF),
@@ -609,7 +653,7 @@
             pltpu.VMEM((4, ROWS, 256), BF),
             pltpu.VMEM((4, 128, 256), F32),
             pltpu.VMEM((4, 128, 256), F32),
-            pltpu.VMEM((6, ROWS, 128), F32),
+            pltpu.VMEM((6, 33 * 16, 128), F32),
             dma((5, 7)),
             dma((5, 7)),
             dma((5, 8)),
@@ -637,7 +681,7 @@
         tokens,
         slide_lengths,
         conv_weight,
-        norm_gain.reshape(1, D),
+        norm_gain,
         w_query,
         w_keyvalue,
         w_out,

time: 79.8 us -> 69 us (0.86)
  the two profiles are of different devices: /device:TPU:64 before, /device:TPU:1 now
where the time goes in v2:
time: 69 us; the launch traced here: 68.6 us
  Pallas kernels  65.8 us (95%)
  local copies, waits for them, and re-layouts  2.06 us (3%)
    pallas_call x1, Pallas kernels, on_device(): pl.pallas_call(kernel, out_shape=jax.ShapeDtypeStruct((1, ROWS, D), BF),...  65.8 us
    unnamed x1, local copies, waits for them, and re-layouts  2.06 us

profile of v2, /device:TPU:1, one launch (start us, length us, event | category | flops | bytes accessed | tf_op | source)
XLA Modules:
  0.0 68.6 jit_solution(14761089891118192664)
XLA Ops:
  0.7 65.8 %layer.1 = bf16[1,512,768]{2,1,0:T(8,128)(2,1)} custom-call(bf16[1,512,768]{2,1,0:T(8,128)(2,1)} %tok_hbm.1, s32[1]{0:T(128)S(6)} %copy.9.len_ref, f32[5,768]{1,0:T(8,128)} %cw_hbm.1, f32[768]{0:T(1024)} %gain_hbm.1, bf16[48,768]{1,0:T(8,128)(2,1)} %wq_hbm.1, bf16[48,1536]{1,0:T(8,128)(2,1)} %wkv_hbm.1, bf16[48,768]{1,0:T(8,128)(2,1)} %wo_hbm.1), custom_call_target="tpu_custom_call" | custom-call | tf_op jit(solution)/shard_map/layer/pallas_call | solution.py:625
  66.5 2.1 %copy.10 = bf16[1,512,768]{2,1,0:T(8,128)(2,1)} copy(bf16[1,512,768]{2,1,0:T(8,128)(2,1)} %layer.1) | data formatting | bytes 1572864

commit v3 on v2

--- a/solution.py
+++ b/solution.py
@@ -43,15 +43,22 @@
 def attend3(qa, qb, kv, bias):
     low = lanes(qa.shape) < HEAD
     zero = jnp.zeros_like(qa)
-    o0, l0 = softmax_block(jnp.where(low, qa, zero), kv(0), bias)
-    o1, l1 = softmax_block(jnp.where(low, zero, qa), kv(1), bias)
-    o2, l2 = softmax_block(qb, kv(2), bias)
-    flow = lanes(o0.shape) < HEAD
+    qs = (jnp.where(low, qa, zero), jnp.where(low, zero, qa), qb)
+    ss = [dot_nt(q, kv(u)) + bias for u, q in enumerate(qs)]
+    ms = [jnp.max(s, axis=1, keepdims=True) for s in ss]
+    es = [jnp.exp(s - m) for s, m in zip(ss, ms)]
+    ts = [jnp.sum(e, axis=1, keepdims=True) for e in es]
+    os = [
+        jnp.dot(e.astype(BF), kv(u), preferred_element_type=F32) / ts[u]
+        for u, e in enumerate(es)
+    ]
+    ls = [m + jnp.log(t) for m, t in zip(ms, ts)]
+    flow = lanes(os[0].shape) < HEAD
     return (
-        jnp.where(flow, o1, o0),
-        jnp.where(flow, 0.0, o2),
-        jnp.where(flow, l1, l0),
-        jnp.broadcast_to(l2, o2.shape),
+        jnp.where(flow, os[1], os[0]),
+        jnp.where(flow, 0.0, os[2]),
+        jnp.where(flow, ls[1], ls[0]),
+        jnp.broadcast_to(ls[2], os[2].shape),
     )
 
 
@@ -101,6 +108,7 @@
     dout,
     dlog,
     outf,
+    pacc,
     ring_s,
     ring_r,
     sib_s,
@@ -324,13 +332,13 @@
         )
     conv_range(0, 6)
     event(1, 2)
+    event(0, 3)
     event(2, 1)
-    event(0, 3)
     event(3, 0)
     conv_range(26, 32)
     event(1, 3)
+    event(0, 4)
     event(2, 2)
-    event(0, 4)
     event(3, 1)
     event(4, 0)
     complete(0)
@@ -363,7 +371,7 @@
     def slz_copy(g):
         return pltpu.make_async_remote_copy(
             src_ref=slp.at[g],
-            dst_ref=sl.at[x, z],
+            dst_ref=sl.at[x, zr, zg],
             send_sem=slz_s.at[g],
             recv_sem=slz_r.at[g],
             device_id=(b, x * NZ + zg * 4 + cls(g)),
@@ -373,19 +381,20 @@
     def slo_copy(g):
         return pltpu.make_async_remote_copy(
             src_ref=slp.at[g],
-            dst_ref=sl.at[x, z],
+            dst_ref=sl.at[x, zr, zg],
             send_sem=slo_s.at[g],
             recv_sem=slo_r.at[g],
             device_id=(b, x * NZ + (1 - zg) * 4 + cls(g)),
             device_id_type=MESH,
         )
 
-    def slx_copy(i):
-        return pltpu.make_async_remote_copy(
-            src_ref=sl.at[x],
-            dst_ref=sl.at[x],
-            send_sem=slx_s.at[i],
-            recv_sem=slx_r.at[i],
+    def slx_copy(g, i):
+        part = sl.at[x, (zr + 3 - g) % 4]
+        return pltpu.make_async_remote_copy(
+            src_ref=part,
+            dst_ref=part,
+            send_sem=slx_s.at[g, i],
+            recv_sem=slx_r.at[g, i],
             device_id=(b, ((x + i + 1) % NX) * NZ + z),
             device_id_type=MESH,
         )
@@ -420,7 +429,7 @@
             tile = kvq[g, rows, 128 * u : 128 * u + 128]
             slp[g, u] = tile
             if g == 3:
-                sl[x, z, u] = tile
+                sl[x, zr, zg, u] = tile
         slo_copy(g).start()
         if g < 3:
             slz_copy(g).start()
@@ -438,23 +447,58 @@
 
     def dense(g, i):
         cg = cls(g)
-        r = (cg + i) % 4
-        rows = pl.ds(pl.multiple_of(r * 128, 128), 128)
+        two = [(cg + 2 * i) % 4, (cg + 2 * i + 1) % 4]
+        rows = [pl.ds(pl.multiple_of(r * 128, 128), 128) for r in two]
         o0, o1, l0, l1 = attend3(
-            kvq[g, rows, 384:512],
-            kvq[g, rows, 512:640],
+            jnp.concatenate([kvq[g, rows[0], 384:512], kvq[g, rows[1], 384:512]], axis=0),
+            jnp.concatenate([kvq[g, rows[0], 512:640], kvq[g, rows[1], 512:640]], axis=0),
             lambda u: kvq[g, :, 128 * u : 128 * u + 128],
             dense_bias,
         )
-        if i == 0:
-            dout[g, :, 0:128] = o0
-            dout[g, :, 128:256] = o1
-            dlog[g, :, 0:128] = l0
-            dlog[g, :, 128:256] = l1
-        else:
-            ok = live(r, 128)
-            attn[cg, rows, 0:128] = jnp.where(ok, o0, 0.0).astype(BF)
-            attn[cg, rows, 128:256] = jnp.where(ok, o1, 0.0).astype(BF)
+        for n in range(2):
+            part = slice(128 * n, 128 * n + 128)
+            if i == 0 and n == 0:
+                dout[g, :, 0:128] = o0[part]
+                dout[g, :, 128:256] = o1[part]
+                dlog[g, :, 0:128] = l0[part]
+                dlog[g, :, 128:256] = l1[part]
+            else:
+                ok = live(two[n], 128)
+                attn[cg, rows[n], 0:128] = jnp.where(ok, o0[part], 0.0).astype(BF)
+                attn[cg, rows[n], 128:256] = jnp.where(ok, o1[part], 0.0).astype(BF)
+
+    group_first = (q // 4) * 4 * ROWS
+    mid_bias = jnp.where(group_first + 512 * (key // 128) + inner + zr < length, 0.0, NEG)
+
+    def middle(pair):
+        gs = (2 * pair, 2 * pair + 1)
+        src = [(zr + 3 - g) % 4 for g in gs]
+        o0, o1, l0, l1 = attend3(
+            jnp.concatenate([mid[m, :, 384:512] for m in src], axis=0),
+            jnp.concatenate([mid[m, :, 512:640] for m in src], axis=0),
+            lambda u: mid[:, :, 128 * u : 128 * u + 128].reshape(ROWS, 128),
+            mid_bias,
+        )
+        lane = lanes(o0.shape)
+        logs = jnp.where(
+            lane < 16, pltpu.roll(l0, HEAD, 1), jnp.where(lane < 32, l0, l1)
+        )
+        logs = jnp.where(lane < 48, split_log(logs, lane), 0.0)
+        o1 = jnp.where(lane < HEAD, logs, o1).astype(BF)
+        o0 = o0.astype(BF)
+        for n, g in enumerate(gs):
+            part = slice(128 * n, 128 * n + 128)
+            oret[g, :, 0:128] = o0[part]
+            oret[g, :, 128:256] = o1[part]
+            if g < 3:
+                ret_copy(g).start()
+
+    def slide_out(g):
+        if g < 3:
+            slz_copy(g).wait_recv()
+        slo_copy(g).wait_recv()
+        for i in range(3):
+            slx_copy(g, i).start()
 
     for g in range(4):
         project(g)
@@ -462,52 +506,40 @@
         event(g + 1, 4)
         dense(g, 0)
         event(g + 2, 3)
+        event(g + 3, 2)
+        if g > 0:
+            slide_out(g - 1)
         dense(g, 1)
-        event(g + 3, 2)
-        dense(g, 2)
         event(g + 4, 1)
-        dense(g, 3)
         if g < 3:
             complete(g + 1)
-
-    for g in range(3):
-        slz_copy(g).wait_recv()
-    for g in range(4):
-        slo_copy(g).wait_recv()
-    for i in range(3):
-        slx_copy(i).start()
-
+    slide_out(3)
     for g in range(3):
         a2a_copy(g).wait_recv()
-    group_first = (q // 4) * 4 * ROWS
-    mid_bias = jnp.where(group_first + 512 * (key // 128) + inner + zr < length, 0.0, NEG)
-
-    def mid_step(g, carry):
-        m = (zr + 3 - g) % 4
-        o0, o1, l0, l1 = attend3(
-            mid[m, :, 384:512],
-            mid[m, :, 512:640],
-            lambda u: mid[:, :, 128 * u : 128 * u + 128].reshape(ROWS, 128),
-            mid_bias,
-        )
-        lane = lanes(o0.shape)
-        logs = jnp.where(
-            lane < 16, pltpu.roll(l0, HEAD, 1), jnp.where(lane < 32, l0, l1)
-        )
-        logs = jnp.where(lane < 48, split_log(logs, lane), 0.0)
-        oret[g, :, 0:128] = o0.astype(BF)
-        oret[g, :, 128:256] = jnp.where(lane < HEAD, logs, o1).astype(BF)
-
-        @pl.when(g < 3)
-        def _():
-            ret_copy(g).start()
-
-        return carry
-
-    lax.fori_loop(0, 4, mid_step, 0)
-
-    for i in range(3):
-        slx_copy(i).wait_recv()
+    middle(0)
+    middle(1)
+
+    complete(4)
+    for r in range(4):
+        woutp[r, 0:64, :] = woutf[HEAD * (r + 4) : HEAD * (r + 5), :]
+        woutp[r, 64:128, :] = woutf[HEAD * r : HEAD * (r + 1), :]
+        woutp[r, 128:192, :] = jnp.zeros((64, D), BF)
+        woutp[r, 192:256, :] = woutf[HEAD * (r + 8) : HEAD * (r + 9), :]
+
+    def partial(g):
+        res = None
+        for k in range(1, 4):
+            r = cls(g + k)
+            term = jnp.dot(attn[r, cls_rows(g), :], woutp[r], preferred_element_type=F32)
+            res = term if res is None else res + term
+        pacc[g] = res
+
+    for g in range(4):
+        partial(g)
+
+    for g in range(4):
+        for i in range(3):
+            slx_copy(g, i).wait_recv()
     lane64 = lanes((64, 128))
     for u in range(3):
         low = 0 if u != 1 else HEAD
@@ -515,8 +547,9 @@
         qs = mid[:, 16 * u : 16 * u + 16, blk].reshape(64, 128)
         mine = jnp.where(low == 0, lane64, lane64 - HEAD + 128) % 128 < HEAD
         qs = jnp.where(mine, qs, jnp.zeros_like(qs))
-        kv = sl[:, :, u].reshape(ROWS, 128)
-        bias = jnp.where(32 * key + 4 * u + zr < length, 0.0, NEG)
+        kv = sl[:, :, :, u].reshape(ROWS, 128)
+        device = NZ * (key // 128) + 4 * ((key // 16) % 2) + (key // 32) % 4
+        bias = jnp.where(512 * device + 32 * (key % 16) + 4 * u + zr < length, 0.0, NEG)
         o, lg = softmax_block(qs, kv, bias)
         logs = split_log(jnp.broadcast_to(lg, o.shape), lane64)
         packed = jnp.where(mine, logs, o).astype(BF)
@@ -525,13 +558,6 @@
     for g in range(3):
         srt_copy(g).start()
 
-    complete(4)
-    for r in range(4):
-        woutp[r, 0:64, :] = woutf[HEAD * (r + 4) : HEAD * (r + 5), :]
-        woutp[r, 64:128, :] = woutf[HEAD * r : HEAD * (r + 1), :]
-        woutp[r, 128:192, :] = jnp.zeros((64, D), BF)
-        woutp[r, 192:256, :] = woutf[HEAD * (r + 8) : HEAD * (r + 9), :]
-
     def join(logs, outs):
         top = jnp.maximum(jnp.maximum(logs[0], logs[1]), logs[2])
         cs = [jnp.exp(lg - top) for lg in logs]
@@ -544,7 +570,6 @@
 
     def finish(g, mret, sr):
         cg = cls(g)
-        rows = cls_rows(g)
         m0 = mret[:, 0:128].astype(F32)
         m1 = mret[:, 128:256].astype(F32)
 
@@ -575,11 +600,10 @@
         a0 = join((dlog[g, :, 0:128], ml0, sl0), (dout[g, :, 0:128], m0, s0))
         a1 = join((dlog[g, :, 128:256], ml1, sl1), (dout[g, :, 128:256], m1, s1))
         a1 = jnp.where(flow, 0.0, a1)
-        attn[cg, rows, 0:128] = jnp.where(ok, a0, 0.0).astype(BF)
-        attn[cg, rows, 128:256] = jnp.where(ok, a1, 0.0).astype(BF)
-        res = jnp.dot(attn[0, rows, :], woutp[0], preferred_element_type=F32)
-        for r in range(1, 4):
-            res = res + jnp.dot(attn[r, rows, :], woutp[r], preferred_element_type=F32)
+        row = jnp.concatenate(
+            [jnp.where(ok, a0, 0.0).astype(BF), jnp.where(ok, a1, 0.0).astype(BF)], axis=1
+        )
+        res = pacc[g] + jnp.dot(row, woutp[cg], preferred_element_type=F32)
         for v in range(8):
             for i in range(6):
                 outf[i, pl.ds(4 * v + cg, 16, stride=33), :] = res[
@@ -600,9 +624,10 @@
     for g in range(3):
         a2a_copy(g).wait_send()
         slz_copy(g).wait_send()
-        slx_copy(g).wait_send()
     for g in range(4):
         slo_copy(g).wait_send()
+        for i in range(3):
+            slx_copy(g, i).wait_send()
 
     for g in range(3):
         ret_copy(g).wait_recv()
@@ -645,7 +670,7 @@
             pltpu.VMEM((4, ROWS, CW), BF),
             pltpu.VMEM((4, 128, CW), BF),
             pltpu.VMEM((4, 3, 16, 128), BF),
-            pltpu.VMEM((NX, NZ, 3, 16, 128), BF),
+            pltpu.VMEM((NX, 4, 2, 3, 16, 128), BF),
             pltpu.VMEM((4, 128, 256), BF),
             pltpu.VMEM((3, 128, 256), BF),
             pltpu.VMEM((4, 3, 16, 128), BF),
@@ -654,6 +679,7 @@
             pltpu.VMEM((4, 128, 256), F32),
             pltpu.VMEM((4, 128, 256), F32),
             pltpu.VMEM((6, 33 * 16, 128), F32),
+            pltpu.VMEM((4, 128, D), F32),
             dma((5, 7)),
             dma((5, 7)),
             dma((5, 8)),
@@ -666,8 +692,8 @@
             dma((3,)),
             dma((4,)),
             dma((4,)),
-            dma((3,)),
-            dma((3,)),
+            dma((4, 3)),
+            dma((4, 3)),
             dma((3,)),
             dma((3,)),
             dma((3,)),

time: 69 us -> 66.4 us (0.962)
  Pallas kernels: 65.8 us -> 63.5 us
    pallas_call x1, Pallas kernels: 65.8 us -> 63.5 us  [on_device(): pl.pallas_call(kernel, out_shape=jax.ShapeDtypeStruct((1, ROWS, D), BF),...]
where the time goes in v3:
time: 66.4 us; the launch traced here: 66.2 us
  Pallas kernels  63.5 us (96%)
  local copies, waits for them, and re-layouts  2.06 us (3%)
    pallas_call x1, Pallas kernels, on_device(): pl.pallas_call(kernel, out_shape=jax.ShapeDtypeStruct((1, ROWS, D), BF),...  63.5 us
    unnamed x1, local copies, waits for them, and re-layouts  2.06 us

profile of v3, /device:TPU:1, one launch (start us, length us, event | category | flops | bytes accessed | tf_op | source)
XLA Modules:
  0.0 66.2 jit_solution(11669269511077199032)
XLA Ops:
  0.7 63.5 %layer.1 = bf16[1,512,768]{2,1,0:T(8,128)(2,1)} custom-call(bf16[1,512,768]{2,1,0:T(8,128)(2,1)} %tok_hbm.1, s32[1]{0:T(128)S(6)} %copy.9.len_ref, f32[5,768]{1,0:T(8,128)} %cw_hbm.1, f32[768]{0:T(1024)} %gain_hbm.1, bf16[48,768]{1,0:T(8,128)(2,1)} %wq_hbm.1, bf16[48,1536]{1,0:T(8,128)(2,1)} %wkv_hbm.1, bf16[48,768]{1,0:T(8,128)(2,1)} %wo_hbm.1), custom_call_target="tpu_custom_call" | custom-call | tf_op jit(solution)/shard_map/layer/pallas_call | solution.py:650
  64.2 2.1 %copy.10 = bf16[1,512,768]{2,1,0:T(8,128)(2,1)} copy(bf16[1,512,768]{2,1,0:T(8,128)(2,1)} %layer.1) | data formatting | bytes 1572864
